TPU v7x, 32 devices: a whole 2x2x4 slice. The times are simulated.
32 devices in a mesh: dp: 4 (over y, x), row: 4 (over z), col: 2 (over core).
Axes of the slice: x: 2, y: 2, z: 4, core: 2. Of those that a mesh axis runs over, the one named last changes fastest.
Arguments:
- image: bfloat16 [4, 256, 96, 256], P('dp', None, 'row', 'col'), may hold values from -6 to 6
- cotangent: bfloat16 [4, 256, 96, 256], P('dp', None, 'row', 'col'), may hold values from -6 to 6
- w_reduce: bfloat16 [256, 64], replicated, may hold values from -0.375 to 0.375
- w_spatial: bfloat16 [3, 3, 64, 64], replicated, may hold values from -0.25 to 0.25
- w_expand: bfloat16 [64, 256], replicated, may hold values from -0.75 to 0.75
Outputs:
- grad_image: bfloat16 [4, 256, 96, 256], P('dp', None, 'row', 'col')
- grad_reduce: float32 [256, 64], replicated
- grad_spatial: float32 [3, 3, 64, 64], replicated
- grad_expand: float32 [64, 256], replicated
All inputs are finite; a program needn't handle non-finite values.
Results may differ from a plain program's by a relative error of at most 0.0061.
Values may be sent and summed in bfloat16 or wider, within the bound.
A program may use at most 64 MiB of HBM per device.

v0:
```python
import jax
import jax.numpy as jnp
from jax import lax
from jax.sharding import PartitionSpec as P

GELU_C = 0.7978845608028654
GELU_K = 0.044715


def padded_2(block, sides, width):
    for axis, dim in sides:
        count = lax.axis_size(axis)
        forward = [(i, i + 1) for i in range(count - 1)]
        backward = [(target, source) for source, target in forward]
        low = lax.ppermute(
            lax.slice_in_dim(block, block.shape[dim] - width, None, axis=dim), axis, forward
        )
        high = lax.ppermute(lax.slice_in_dim(block, 0, width, axis=dim), axis, backward)
        block = jnp.concatenate([low, block, high], axis=dim)
    return block


def gelu(v):
    t = jnp.tanh(GELU_C * (v + GELU_K * v * v * v))
    return 0.5 * v * (1.0 + t)


def slope(v):
    t = jnp.tanh(GELU_C * (v + GELU_K * v * v * v))
    return 0.5 * (1.0 + t) + 0.5 * v * (1.0 - t * t) * GELU_C * (1.0 + 3.0 * GELU_K * v * v)


def stacked_taps(padded, height, width, flipped):
    pieces = []
    for row_k in range(3):
        for col_k in range(3):
            if flipped:
                pieces.append(
                    padded[:, 2 - row_k : 2 - row_k + height, 2 - col_k : 2 - col_k + width]
                )
            else:
                pieces.append(padded[:, row_k : row_k + height, col_k : col_k + width])
    return jnp.concatenate(pieces, axis=0)


def body(image, cotangent, w_reduce, w_spatial, w_expand):
    feats = image[0]
    upstream = cotangent[0]
    channels, height, width = feats.shape
    inner = w_reduce.shape[1]
    pixels = height * width * lax.axis_size("dp") * lax.axis_size("row") * lax.axis_size("col")
    scale = float(pixels) ** (-0.5)
    f32 = jnp.float32
    pre_one = jnp.einsum("chw,cm->mhw", feats, w_reduce, preferred_element_type=f32)
    hidden_one = gelu(pre_one).astype(jnp.bfloat16)
    pad_one = padded_2(hidden_one, (("row", 1), ("col", 2)), 1)
    patches = stacked_taps(pad_one, height, width, False)
    spatial_flat = w_spatial.reshape(9 * inner, inner)
    pre_two = jnp.einsum("khw,kd->dhw", patches, spatial_flat, preferred_element_type=f32)
    hidden_two = gelu(pre_two).astype(jnp.bfloat16)
    total = jnp.einsum(
        "mhw,mc->chw", hidden_two, w_expand, preferred_element_type=f32
    ) + feats.astype(f32)
    top = (upstream.astype(f32) * slope(total)).astype(jnp.bfloat16)
    grad_expand = jnp.einsum("mhw,chw->mc", hidden_two, top, preferred_element_type=f32) * scale
    back_two = (
        jnp.einsum("chw,mc->mhw", top, w_expand, preferred_element_type=f32) * slope(pre_two)
    ).astype(jnp.bfloat16)
    pad_back = padded_2(back_two, (("row", 1), ("col", 2)), 1)
    grad_spatial = (
        jnp.einsum("khw,dhw->kd", patches, back_two, preferred_element_type=f32).reshape(
            3, 3, inner, inner
        )
        * scale
    )
    back_taps = stacked_taps(pad_back, height, width, True)
    spatial_turned = jnp.transpose(w_spatial, (0, 1, 3, 2)).reshape(9 * inner, inner)
    back_pre = jnp.einsum("khw,kc->chw", back_taps, spatial_turned, preferred_element_type=f32)
    back_one = (back_pre * slope(pre_one)).astype(jnp.bfloat16)
    grad_reduce = jnp.einsum("chw,mhw->cm", feats, back_one, preferred_element_type=f32) * scale
    result = (
        jnp.einsum("mhw,cm->chw", back_one, w_reduce, preferred_element_type=f32) + top.astype(f32)
    ).astype(jnp.bfloat16)
    grad_reduce, grad_spatial, grad_expand = lax.psum(
        (grad_reduce, grad_spatial, grad_expand), ("dp", "row", "col")
    )
    return (result.reshape(1, channels, height, width), grad_reduce, grad_spatial, grad_expand)


def solution(mesh):
    in_specs = (P("dp", None, "row", "col"), P("dp", None, "row", "col"), P(), P(), P())
    out_specs = (P("dp", None, "row", "col"), P(), P(), P())
    return jax.shard_map(body, mesh=mesh, in_specs=in_specs, out_specs=out_specs, check_vma=False)
```

profile of v0, /device:TPU:0, one launch (start us, length us, event | category | flops | bytes accessed | tf_op | source)
XLA Modules:
  0.0 198.6 jit_solution(10238605451038991250)
XLA Ops:
  7.2 2.2 %copy.29 = bf16[256,24,128]{0,2,1:T(8,128)(2,1)S(1)} copy(bf16[256,24,128]{2,1,0:T(8,128)(2,1)} %bitcast.81) | data formatting | bytes 3145728 | tf_op jit(solution)/shard_map/squeeze | solution.py:47
  9.4 1.5 multiply_convert_fusion.1
  10.9 4.9 %collective-permute-start = (bf16[64,1,128]{2,0,1:T(8,128)(2,1)S(1)}, bf16[64,1,128]{2,0,1:T(8,128)(2,1)S(1)}, u32[]{:S(2)}, u32[]{:S(2)}) collective-permute-start(bf16[64,1,128]{2,0,1:T(8,128)(2,1)S(1)} %get-tuple-element.25), channel_id=1, source_target_pairs={{0,2},{2,4},{4,6},{1,3},{3,5},{5,7},{8,10},{10,12},{12,14},{9,11},... | collective-permute-start | bytes 49160 | tf_op jit(solution)/shard_map/ppermute | solution.py:15
  15.8 1.3 collective-permute-start.1
  17.3 4.2 %collective-permute-done.1 = bf16[64,1,128]{2,0,1:T(8,128)(2,1)S(1)} collective-permute-done((bf16[64,1,128]{2,0,1:T(8,128)(2,1)S(1)}, bf16[64,1,128]{2,0,1:T(8,128)(2,1)S(1)}, u32[]{:S(2)}, u32[]{:S(2)}) %collective-permute-start.1) | collective-permute-done | bytes 16416 | tf_op jit(solution)/shard_map/ppermute | solution.py:18
  22.5 1.3 collective-permute-start.2
  23.9 1.4 collective-permute-start.3
  25.3 2.9 %copy.19 = bf16[1,256,24,128]{1,3,2,0:T(8,128)(2,1)} copy(bf16[1,256,24,128]{3,2,1,0:T(8,128)(2,1)} %param.5) | data formatting | bytes 3145728 | tf_op args[0]
  28.2 2.8 %copy.18 = bf16[1,256,24,128]{1,3,2,0:T(8,128)(2,1)} copy(bf16[1,256,24,128]{3,2,1,0:T(8,128)(2,1)} %param.6) | data formatting | bytes 3145728 | tf_op args[1]
  35.1 2.7 %fusion.6 = bf16[256,24,128]{0,2,1:T(8,128)(2,1)S(1)} fusion(bf16[1,256,24,128]{1,3,2,0:T(8,128)(2,1)S(1)} %copy-done.4, bf16[1,256,24,128]{1,3,2,0:T(8,128)(2,1)S(1)} %copy-done.3, bf16[64,256]{1,0:T(8,128)(2,1)S(1)} %copy-done.9, f32[64,24,128]{2,0,1:T(8,128)S(1)} %convolution_bitcast_fusion.2), kind=kOutput, calls=%fused_computation.8 | convolution fusion | flops 119734272 | bytes 5537792 | tf_op jit(solution)/shard_map/mhw,mc->chw/dot_general | solution.py:61
  38.6 3.5 %collective-permute-start.4 = (bf16[64,1,128]{2,0,1:T(8,128)(2,1)S(1)}, bf16[64,1,128]{2,0,1:T(8,128)(2,1)S(1)}, u32[]{:S(2)}, u32[]{:S(2)}) collective-permute-start(bf16[64,1,128]{2,0,1:T(8,128)(2,1)S(1)} %get-tuple-element.23), channel_id=1, source_target_pairs={{0,2},{2,4},{4,6},{1,3},{3,5},{5,7},{8,10},{10,12},{12,14},{9,11},... | collective-permute-start | bytes 49160 | tf_op jit(solution)/shard_map/ppermute | solution.py:15
  42.1 1.3 collective-permute-start.5
  43.4 1.2 fusion.13
  44.6 3.2 %collective-permute-done.5 = bf16[64,1,128]{2,0,1:T(8,128)(2,1)S(1)} collective-permute-done((bf16[64,1,128]{2,0,1:T(8,128)(2,1)S(1)}, bf16[64,1,128]{2,0,1:T(8,128)(2,1)S(1)}, u32[]{:S(2)}, u32[]{:S(2)}) %collective-permute-start.5) | collective-permute-done | bytes 16416 | tf_op jit(solution)/shard_map/ppermute | solution.py:18
  48.8 1.3 collective-permute-start.6
  50.1 3.3 %collective-permute-start.7 = (bf16[64,26,1]{2,0,1:T(8,128)(2,1)S(1)}, bf16[64,26,1]{2,0,1:T(8,128)(2,1)S(1)}, u32[]{:S(2)}, u32[]{:S(2)}) collective-permute-start(bf16[64,26,1]{2,0,1:T(8,128)(2,1)S(1)} %get-tuple-element.17), channel_id=1, source_target_pairs={{0,1},{2,3},{4,5},{6,7},{8,9},{10,11},{12,13},{14,15},{16,17},{18,... | collective-permute-start | bytes 9992 | tf_op jit(solution)/shard_map/ppermute | solution.py:15
  53.4 1.1 fusion.14
  57.2 1.2 fusion.11
  59.5 1.6 fusion.8
  61.1 1.9 copy.28
  63.0 124.1 %all-reduce.3.cloned.1.call-done = (f32[256,64]{0,1:T(8,128)}, f32[3,3,64,64]{3,2,1,0:T(8,128)}, f32[64,256]{1,0:T(8,128)}) async-done(((f32[256,64]{0,1:T(8,128)}, f32[3,3,64,64]{3,2,1,0:T(8,128)}, f32[64,256]{1,0:T(8,128)}), (f32[256,64]{0,1:T(8,128)}, f32[3,3,64,64]{3,2,1,0:T(8,128)}, f32[64,256]{1,0:T(8,128)})) %all-reduce.3.cloned.1.call-update) | async-done | bytes 278544 | tf_op jit(solution)/shard_map/psum | solution.py:84
  187.1 1.5 copy.60
  188.6 1.7 copy.61
  190.3 1.5 copy.62
  (59 shorter events, 10.8 us)
Async XLA Ops:
  7.2 2.2 %copy-start = (bf16[256,64]{0,1:T(8,128)(2,1)S(1)}, bf16[256,64]{0,1:T(8,128)(2,1)}, u32[]{:S(2)}) copy-start(bf16[256,64]{0,1:T(8,128)(2,1)} %param.7) | copy-start | bytes 98308
  7.2 179.9 %all-reduce.3.cloned.1.call-start = ((), (), s32[]{:S(2)}) async-start(), calls=%async_computation | async-start | bytes 851968 | tf_op jit(solution)/shard_map/psum | solution.py:84
  10.9 6.4 %collective-permute-start = (bf16[64,1,128]{2,0,1:T(8,128)(2,1)S(1)}, bf16[64,1,128]{2,0,1:T(8,128)(2,1)S(1)}, u32[]{:S(2)}, u32[]{:S(2)}) collective-permute-start(bf16[64,1,128]{2,0,1:T(8,128)(2,1)S(1)} %get-tuple-element.25), channel_id=1, source_target_pairs={{0,2},{2,4},{4,6},{1,3},{3,5},{5,7},{8,10},{10,12},{12,14},{9,11},... | collective-permute-start | bytes 49160 | tf_op jit(solution)/shard_map/ppermute | solution.py:15
  15.8 5.6 %collective-permute-start.1 = (bf16[64,1,128]{2,0,1:T(8,128)(2,1)S(1)}, bf16[64,1,128]{2,0,1:T(8,128)(2,1)S(1)}, u32[]{:S(2)}, u32[]{:S(2)}) collective-permute-start(bf16[64,1,128]{2,0,1:T(8,128)(2,1)S(1)} %get-tuple-element.26), channel_id=1, source_target_pairs={{2,0},{4,2},{6,4},{3,1},{5,3},{7,5},{10,8},{12,10},{14,12},{11,9},... | collective-permute-start | bytes 49160 | tf_op jit(solution)/shard_map/ppermute | solution.py:18
  22.5 9.2 %collective-permute-start.2 = (bf16[64,26,1]{2,0,1:T(8,128)(2,1)}, bf16[64,26,1]{2,0,1:T(8,128)(2,1)S(1)}, u32[]{:S(2)}, u32[]{:S(2)}) collective-permute-start(bf16[64,26,1]{2,0,1:T(8,128)(2,1)} %get-tuple-element.22), channel_id=1, source_target_pairs={{0,1},{2,3},{4,5},{6,7},{8,9},{10,11},{12,13},{14,15},{16,17},{18,... | collective-permute-start | bytes 9992 | tf_op jit(solution)/shard_map/ppermute | solution.py:15
  23.8 7.1 %copy-start.7 = (bf16[3,3,64,64]{3,2,1,0:T(8,128)(2,1)S(1)}, bf16[3,3,64,64]{3,2,1,0:T(8,128)(2,1)}, u32[]{:S(2)}) copy-start(bf16[3,3,64,64]{3,2,1,0:T(8,128)(2,1)} %param.8) | copy-start | bytes 221188
  23.9 7.9 %collective-permute-start.3 = (bf16[64,26,1]{2,0,1:T(8,128)(2,1)S(1)}, bf16[64,26,1]{2,0,1:T(8,128)(2,1)S(1)}, u32[]{:S(2)}, u32[]{:S(2)}) collective-permute-start(bf16[64,26,1]{2,0,1:T(8,128)(2,1)S(1)} %get-tuple-element.21), channel_id=1, source_target_pairs={{1,0},{3,2},{5,4},{7,6},{9,8},{11,10},{13,12},{15,14},{17,16},{19,... | collective-permute-start | bytes 9992 | tf_op jit(solution)/shard_map/ppermute | solution.py:18
  33.2 1.4 copy-start.3
  33.2 1.9 copy-start.4
  33.2 1.9 copy-start.9
  37.8 15.5 %copy-start.1 = (bf16[256,24,128]{0,2,1:T(8,128)(2,1)}, bf16[256,24,128]{0,2,1:T(8,128)(2,1)S(1)}, u32[]{:S(2)}) copy-start(bf16[256,24,128]{0,2,1:T(8,128)(2,1)S(1)} %fusion.6) | copy-start | bytes 4718596
  38.6 6.0 %collective-permute-start.4 = (bf16[64,1,128]{2,0,1:T(8,128)(2,1)S(1)}, bf16[64,1,128]{2,0,1:T(8,128)(2,1)S(1)}, u32[]{:S(2)}, u32[]{:S(2)}) collective-permute-start(bf16[64,1,128]{2,0,1:T(8,128)(2,1)S(1)} %get-tuple-element.23), channel_id=1, source_target_pairs={{0,2},{2,4},{4,6},{1,3},{3,5},{5,7},{8,10},{10,12},{12,14},{9,11},... | collective-permute-start | bytes 49160 | tf_op jit(solution)/shard_map/ppermute | solution.py:15
  42.1 5.7 %collective-permute-start.5 = (bf16[64,1,128]{2,0,1:T(8,128)(2,1)S(1)}, bf16[64,1,128]{2,0,1:T(8,128)(2,1)S(1)}, u32[]{:S(2)}, u32[]{:S(2)}) collective-permute-start(bf16[64,1,128]{2,0,1:T(8,128)(2,1)S(1)} %get-tuple-element.24), channel_id=1, source_target_pairs={{2,0},{4,2},{6,4},{3,1},{5,3},{7,5},{10,8},{12,10},{14,12},{11,9},... | collective-permute-start | bytes 49160 | tf_op jit(solution)/shard_map/ppermute | solution.py:18
  48.8 6.5 %collective-permute-start.6 = (bf16[64,26,1]{2,0,1:T(8,128)(2,1)}, bf16[64,26,1]{2,0,1:T(8,128)(2,1)S(1)}, u32[]{:S(2)}, u32[]{:S(2)}) collective-permute-start(bf16[64,26,1]{2,0,1:T(8,128)(2,1)} %get-tuple-element.18), channel_id=1, source_target_pairs={{1,0},{3,2},{5,4},{7,6},{9,8},{11,10},{13,12},{15,14},{17,16},{19,... | collective-permute-start | bytes 9992 | tf_op jit(solution)/shard_map/ppermute | solution.py:18
  50.1 5.2 %collective-permute-start.7 = (bf16[64,26,1]{2,0,1:T(8,128)(2,1)S(1)}, bf16[64,26,1]{2,0,1:T(8,128)(2,1)S(1)}, u32[]{:S(2)}, u32[]{:S(2)}) collective-permute-start(bf16[64,26,1]{2,0,1:T(8,128)(2,1)S(1)} %get-tuple-element.17), channel_id=1, source_target_pairs={{0,1},{2,3},{4,5},{6,7},{8,9},{10,11},{12,13},{14,15},{16,17},{18,... | collective-permute-start | bytes 9992 | tf_op jit(solution)/shard_map/ppermute | solution.py:15
  56.1 1.1 copy-start.6
  56.1 1.1 copy-start.8
  57.2 2.2 %copy-start.2 = (bf16[256,24,128]{0,2,1:T(8,128)(2,1)S(1)}, bf16[256,24,128]{0,2,1:T(8,128)(2,1)}, u32[]{:S(2)}) copy-start(bf16[256,24,128]{0,2,1:T(8,128)(2,1)} %copy-done.1) | copy-start | bytes 4718596
  58.4 1.0 copy-start.5
Sparse Core Ops, SparseCore 0:
  59.6 127.4 all-reduce.2
where the time goes:
time: 199 us
  waiting for transfers between devices  132 us (66%)
  local copies, waits for them, and re-layouts  20.8 us (10%)
  starting transfers between devices  18.3 us (9%)
  between operations  14.4 us (7%)
  matrix products  11.8 us (6%)
    psum x1, waiting for transfers between devices, body(): lax.psum((grad_reduce, grad_spatial, grad_expand), ('dp', 'row', 'col'))  124 us
    unnamed x38, local copies, waits for them, and re-layouts  14.8 us
    ppermute x4, starting transfers between devices, padded_2(): lax.ppermute(lax.slice_in_dim(block, block.shape[dim] - width, None, axis...  13 us
    ppermute x4, waiting for transfers between devices, padded_2(): lax.ppermute(lax.slice_in_dim(block, 0, width, axis=dim), axis, backward)  7.43 us
    ppermute x4, starting transfers between devices, padded_2(): lax.ppermute(lax.slice_in_dim(block, 0, width, axis=dim), axis, backward)  5.29 us
  transfers between devices with their start and end apart: 9, of which 4 were waited for; matrix products, arithmetic and copies ran while one was open for 7% of the time, Pallas kernels for 0%

commit v1 on v0

v1 whole, which is shorter than its diff:
```python
import functools

import jax
import jax.numpy as jnp
from jax import lax
from jax.experimental import pallas as pl
from jax.experimental.pallas import tpu as pltpu
from jax.sharding import PartitionSpec as P

GELU_C = 0.7978845608028654
GELU_K = 0.044715
F32 = jnp.float32
BF16 = jnp.bfloat16
AROUND = ((-1, 0), (1, 0), (-1, -1), (0, -1), (1, -1), (-1, 1), (0, 1), (1, 1))
R = 2


def gelu_slope(v):
    v2 = v * v
    t = jnp.tanh(GELU_C * (v + GELU_K * v2 * v))
    half = 0.5 * (1.0 + t)
    return v * half, half + 0.5 * v * (1.0 - t * t) * (GELU_C * (1.0 + 3.0 * GELU_K * v2))


def slope(v):
    return gelu_slope(v)[1]


def dot(a, b):
    return lax.dot_general(a, b, (((1,), (0,)), ((), ())), preferred_element_type=F32)


def dot_nt(a, b):
    return lax.dot_general(a, b, (((1,), (1,)), ((), ())), preferred_element_type=F32)


def kernel(sizes, image, cot, wr, wrt, w2, w3, we, wet, out, g_reduce, g_spatial, g_expand,
           xin, cin, xf, cf, xb, tb, s1, hid, back, edge, rows_in, cols_in,
           in_sem, send_sem, recv_sem):
    nrow, ncol = sizes
    channels, height, width = image.shape
    inner = we.shape[0]
    row, col = lax.axis_index("row"), lax.axis_index("col")
    lane = lax.broadcasted_iota(jnp.int32, (inner, width), 1)

    copy_x = pltpu.make_async_copy(image, xin, in_sem.at[0])
    copy_c = pltpu.make_async_copy(cot, cin, in_sem.at[1])
    copy_x.start()
    copy_c.start()

    def exists(dr, dc):
        ok = jnp.bool_(True)
        if dr:
            ok = jnp.logical_and(ok, (row > 0) if dr < 0 else (row < nrow - 1))
        if dc:
            ok = jnp.logical_and(ok, (col > 0) if dc < 0 else (col < ncol - 1))
        return ok

    barrier = pltpu.get_barrier_semaphore()
    for dr, dc in AROUND:
        @pl.when(exists(dr, dc))
        def _(dr=dr, dc=dc):
            pl.semaphore_signal(barrier, inc=1, device_id={"row": row + dr, "col": col + dc},
                                device_id_type=pl.DeviceIdType.MESH)
    pl.semaphore_wait(barrier, sum(exists(dr, dc).astype(jnp.int32) for dr, dc in AROUND))

    def halo_copy(turn, k, source):
        dr, dc = AROUND[k]
        if dc == 0:
            src = source.at[1 if dr < 0 else height, pl.ds(inner, inner)]
            dst = rows_in.at[turn, 1 if dr < 0 else 0]
        else:
            src = edge.at[turn, 0 if dc < 0 else 1]
            dst = cols_in.at[turn, 1 if dc < 0 else 0, 1 - dr]
        return pltpu.make_async_remote_copy(
            src_ref=src, dst_ref=dst, send_sem=send_sem.at[turn, k], recv_sem=recv_sem.at[turn, k],
            device_id={"row": row + dr, "col": col + dc}, device_id_type=pl.DeviceIdType.MESH)

    def halo_start(turn, source):
        for k, (dr, dc) in enumerate(AROUND):
            @pl.when(exists(dr, dc))
            def _(k=k):
                halo_copy(turn, k, source).start()

    def halo_wait(turn, source):
        for k, (dr, dc) in enumerate(AROUND):
            here = exists(-dr, -dc)

            @pl.when(here)
            def _(k=k):
                halo_copy(turn, k, source).wait_recv()

            @pl.when(jnp.logical_not(here))
            def _(dr=dr, dc=dc):
                if dc == 0:
                    rows_in[turn, 1 if dr < 0 else 0] = jnp.zeros((inner, width), BF16)
                else:
                    cols_in[turn, 1 if dc < 0 else 0, 1 - dr] = jnp.zeros((inner, width), F32)

        for k, (dr, dc) in enumerate(AROUND):
            @pl.when(exists(dr, dc))
            def _(k=k):
                halo_copy(turn, k, source).wait_send()

    def note_edges(turn, h, value):
        here = lane == h
        edge[turn, 0] = jnp.where(here, pltpu.roll(value, h, 1), edge[turn, 0])
        edge[turn, 1] = jnp.where(here, pltpu.roll(value, h + 1, 1), edge[turn, 1])

    def spread(turn, target):
        target[0, pl.ds(inner, inner)] = rows_in[turn, 0]
        target[height + 1, pl.ds(inner, inner)] = rows_in[turn, 1]
        sides = []
        for side in range(2):
            mid = pltpu.roll(cols_in[turn, side, 1], 1, 1)
            top_row = pltpu.roll(cols_in[turn, side, 0], width - height + 1, 1)
            low_row = pltpu.roll(cols_in[turn, side, 2], height + 1, 1)
            edge[turn, side] = jnp.where(lane == 0, top_row, jnp.where(lane == height + 1, low_row, mid))

        def one(p, _):
            value = target[p, pl.ds(inner, inner)].astype(F32)
            left = jnp.where(lane == 0, pltpu.roll(edge[turn, 0], lax.rem(width - p, width), 1),
                             pltpu.roll(value, 1, 1))
            right = jnp.where(lane == width - 1, pltpu.roll(edge[turn, 1], width - 1 - p, 1),
                              pltpu.roll(value, width - 1, 1))
            target[p, pl.ds(0, inner)] = left.astype(BF16)
            target[p, pl.ds(2 * inner, inner)] = right.astype(BF16)
            return 0

        lax.fori_loop(0, height + 2, one, 0)

    def joined(pieces):
        return jnp.concatenate(pieces, axis=1)

    def patch(source, h):
        return joined([source[pl.ds(h + r, 3)].reshape(9 * inner, width) for r in range(R)])

    def part(value, r):
        return value[:, r * width:(r + 1) * width]

    edge[...] = jnp.zeros_like(edge)
    tiles = 8

    def widen(src, dst):
        def one(i, _):
            block = src[pl.ds(i * tiles, tiles)].astype(F32)
            dst[pl.ds(pl.multiple_of(i * tiles * height, tiles * height), tiles * height)] = block.reshape(tiles * height, width)
            return 0

        lax.fori_loop(0, channels // tiles, one, 0)

    copy_x.wait()
    widen(xin, xf)

    def first(i, _):
        h = i * R
        pieces = []
        for r in range(R):
            piece = xf[pl.ds(h + r, channels, stride=height), :].astype(BF16)
            xb[h + r] = piece
            pieces.append(piece)
        value, grad = gelu_slope(dot(wrt[...], joined(pieces)))
        value = value.astype(BF16)
        for r in range(R):
            s1[h + r] = part(grad, r)
            hid[h + r + 1, pl.ds(inner, inner)] = part(value, r)
            note_edges(0, h + r, part(value, r).astype(F32))
        return 0

    lax.fori_loop(0, height // R, first, 0)
    halo_start(0, hid)
    copy_c.wait()
    widen(cin, cf)
    g_expand[...] = jnp.zeros_like(g_expand)
    g_spatial[...] = jnp.zeros_like(g_spatial)
    g_reduce[...] = jnp.zeros_like(g_reduce)
    halo_wait(0, hid)
    spread(0, hid)

    def second(i, _):
        h = i * R
        value, grad = gelu_slope(dot(w2[...], patch(hid, h)))
        value = value.astype(BF16)
        total = dot(wet[...], value) + joined([xb[h + r] for r in range(R)]).astype(F32)
        given = joined([cf[pl.ds(h + r, channels, stride=height), :] for r in range(R)])
        top = (given * slope(total)).astype(BF16)
        for r in range(R):
            tb[h + r] = part(top, r)
        g_expand[...] += dot_nt(value, top)
        behind = (dot(we[...], top) * grad).astype(BF16)
        for r in range(R):
            back[h + r + 1, pl.ds(inner, inner)] = part(behind, r)
            note_edges(1, h + r, part(behind, r).astype(F32))
        return 0

    lax.fori_loop(0, height // R, second, 0)
    halo_start(1, back)

    def third(i, _):
        h = i * R
        mine = joined([back[h + r + 1, pl.ds(inner, inner)] for r in range(R)])
        g_spatial[...] += dot_nt(patch(hid, h), mine)
        return 0

    lax.fori_loop(0, height // R, third, 0)
    halo_wait(1, back)
    spread(1, back)

    def fourth(i, _):
        h = i * R
        pre = dot(w3[...], patch(back, h))
        grad = joined([s1[h + r] for r in range(R)])
        one = (pre * grad).astype(BF16)
        g_reduce[...] += dot_nt(joined([xb[h + r] for r in range(R)]), one)
        result = dot(wr[...], one) + joined([tb[h + r] for r in range(R)]).astype(F32)
        for r in range(R):
            xf[pl.ds(h + r, channels, stride=height), :] = part(result, r)
        return 0

    lax.fori_loop(0, height // R, fourth, 0)

    def narrow(i, _):
        block = xf[pl.ds(pl.multiple_of(i * tiles * height, tiles * height), tiles * height)]
        out[pl.ds(i * tiles, tiles)] = block.reshape(tiles, height, width).astype(BF16)
        return 0

    lax.fori_loop(0, channels // tiles, narrow, 0)


def body(sizes, image, cotangent, w_reduce, w_spatial, w_expand):
    _, channels, height, width = image.shape
    inner = w_reduce.shape[1]
    count = lax.axis_size("dp") * lax.axis_size("row") * lax.axis_size("col")
    scale = float(height * width * count) ** (-0.5)
    w2 = w_spatial.reshape(9 * inner, inner).T
    w3 = jnp.transpose(w_spatial[::-1, ::-1], (2, 0, 1, 3)).reshape(inner, 9 * inner)
    vmem = pl.BlockSpec(memory_space=pltpu.VMEM)
    hbm = pl.BlockSpec(memory_space=pl.ANY)
    result, g_reduce, g_spatial, g_expand = pl.pallas_call(
        functools.partial(kernel, sizes),
        out_shape=(
            jax.ShapeDtypeStruct((channels, height, width), BF16),
            jax.ShapeDtypeStruct((channels, inner), F32),
            jax.ShapeDtypeStruct((9 * inner, inner), F32),
            jax.ShapeDtypeStruct((inner, channels), F32),
        ),
        in_specs=[hbm, hbm] + [vmem] * 6,
        out_specs=(vmem,) * 4,
        scratch_shapes=[
            pltpu.VMEM((channels, height, width), BF16),
            pltpu.VMEM((channels, height, width), BF16),
            pltpu.VMEM((channels * height, width), F32),
            pltpu.VMEM((channels * height, width), F32),
            pltpu.VMEM((height, channels, width), BF16),
            pltpu.VMEM((height, channels, width), BF16),
            pltpu.VMEM((height, inner, width), F32),
            pltpu.VMEM((height + 2, 3 * inner, width), BF16),
            pltpu.VMEM((height + 2, 3 * inner, width), BF16),
            pltpu.VMEM((2, 2, inner, width), F32),
            pltpu.VMEM((2, 2, inner, width), BF16),
            pltpu.VMEM((2, 2, 3, inner, width), F32),
            pltpu.SemaphoreType.DMA((2,)),
            pltpu.SemaphoreType.DMA((2, len(AROUND))),
            pltpu.SemaphoreType.DMA((2, len(AROUND))),
        ],
        compiler_params=pltpu.CompilerParams(
            collective_id=0, has_side_effects=True, vmem_limit_bytes=48 * 1024 * 1024),
    )(image[0], cotangent[0], w_reduce, w_reduce.T, w2, w3, w_expand, w_expand.T)
    g_reduce, g_spatial, g_expand = lax.psum(
        (g_reduce * scale, g_spatial.reshape(3, 3, inner, inner) * scale, g_expand * scale),
        ("dp", "row", "col"))
    return result[None], g_reduce, g_spatial, g_expand


def solution(mesh):
    sizes = (mesh.shape["row"], mesh.shape["col"])
    in_specs = (P("dp", None, "row", "col"), P("dp", None, "row", "col"), P(), P(), P())
    out_specs = (P("dp", None, "row", "col"), P(), P(), P())
    return jax.shard_map(functools.partial(body, sizes), mesh=mesh, in_specs=in_specs,
                         out_specs=out_specs, check_vma=False)
```

time: 199 us -> 192 us (0.965)
  Pallas kernels: 0 us -> 33.9 us
  starting transfers between devices: 18.3 us -> 0.04 us
  matrix products: 11.8 us -> 0 us
  local copies, waits for them, and re-layouts: 20.8 us -> 12.4 us
  waiting for transfers between devices: 132 us -> 129 us
    pallas_call x0 -> x1, Pallas kernels: none -> 33.9 us  [body(): pl.pallas_call(functools.partial(kernel, sizes), out_shape=(jax.ShapeDtyp...]
    ppermute x8 -> x0, starting transfers between devices: 18.3 us -> none  [the longest x4 13 us: padded_2(): lax.ppermute(lax.slice_in_dim(block, block.shape[dim] - width, None, axis...]
    dot_general x9 -> x0, matrix products: 11.8 us -> none  [the longest x1 2.75 us: body(): jnp.einsum('mhw,mc->chw', hidden_two, w_expand, preferred_element_type=f32)]
    ppermute x8 -> x0, waiting for transfers between devices: 7.56 us -> none  [the longest x4 7.43 us: padded_2(): lax.ppermute(lax.slice_in_dim(block, 0, width, axis=dim), axis, backward)]
    psum x1, waiting for transfers between devices: 124 us -> 129 us  [body(): lax.psum((g_reduce * scale, g_spatial.reshape(3, 3, inner, inner) * scale...]
    unnamed x38 -> x18, local copies, waits for them, and re-layouts: 14.8 us -> 10.2 us
    squeeze x1 -> x0, local copies, waits for them, and re-layouts: 2.15 us -> none  [body(): feats = image[0]]
    mul x0 -> x3, other arithmetic: none -> 2.04 us  [the longest x1 0.74 us: body(): g_spatial.reshape(3, 3, inner, inner) * scale]
  transfers between devices with their start and end apart: 9 -> 1, of which waited for: 4 -> 1; matrix products, arithmetic and copies ran while one was open for 7% -> 0% of each run, Pallas kernels for 0% -> 0%
where the time goes in v1:
time: 192 us
  waiting for transfers between devices  129 us (67%)
  Pallas kernels  33.9 us (18%)
  between operations  14.1 us (7%)
  local copies, waits for them, and re-layouts  12.4 us (6%)
  other arithmetic  2.04 us (1%)
    psum x1, waiting for transfers between devices, body(): lax.psum((g_reduce * scale, g_spatial.reshape(3, 3, inner, inner) * scale...  129 us
    pallas_call x1, Pallas kernels, body(): pl.pallas_call(functools.partial(kernel, sizes), out_shape=(jax.ShapeDtyp...  33.9 us
    unnamed x18, local copies, waits for them, and re-layouts  10.2 us
  transfers between devices with their start and end apart: 1, of which 1 were waited for; matrix products, arithmetic and copies ran while one was open for 0% of the time, Pallas kernels for 0%

profile of v1, /device:TPU:0, one launch (start us, length us, event | category | flops | bytes accessed | tf_op | source)
XLA Modules:
  0.0 191.5 jit_solution(9710612079127057313)
XLA Ops:
  7.2 0.0 all-reduce.3.cloned.1.call-start
  7.2 0.9 reverse_bitcast_fusion
  8.1 0.1 copy.15
  8.3 0.1 copy.18.w3
  8.4 1.0 copy.14
  9.5 0.9 copy.16
  10.4 0.9 copy.17.wr
  11.2 0.0 copy-start
  11.2 1.4 copy-done
  12.6 1.4 copy-done.1
  14.1 0.8 copy-done.2
  14.8 0.8 copy-done.3
  15.6 33.9 %shard_map.84 = (bf16[256,24,128]{2,1,0:T(8,128)(2,1)S(1)}, f32[256,64]{1,0:T(8,128)S(1)}, f32[576,64]{1,0:T(8,128)S(1)}, f32[64,256]{1,0:T(8,128)S(1)}) custom-call(bf16[256,24,128]{2,1,0:T(8,128)(2,1)S(1)} %bitcast.11, bf16[256,24,128]{2,1,0:T(8,128)(2,1)S(1)} %bitcast.12, bf16[256,64]{1,0:T(8,128)(2,1)S(1)} %copy.17.wr, bf16[64,256]{1,0:T(8,128)(2,1)S(1)} %bitcast.16, ...), custom_call_target="tpu_custom_call" | custom-call | tf_op jit(solution)/shard_map/pallas_call | solution.py:239
  49.5 0.7 broadcast_multiply_fusion
  50.3 0.7 broadcast_multiply_fusion.1
  50.9 0.6 broadcast_multiply_fusion.2
  51.6 0.0 all-reduce.3.cloned.1.call-update
  51.6 129.0 %all-reduce.3.cloned.1.call-done = (f32[256,64]{1,0:T(8,128)}, f32[3,3,64,64]{3,2,1,0:T(8,128)}, f32[64,256]{1,0:T(8,128)}) async-done(((f32[256,64]{1,0:T(8,128)}, f32[3,3,64,64]{3,2,1,0:T(8,128)}, f32[64,256]{1,0:T(8,128)}), (f32[256,64]{1,0:T(8,128)}, f32[3,3,64,64]{3,2,1,0:T(8,128)}, f32[64,256]{1,0:T(8,128)})) %all-reduce.3.cloned.1.call-update) | async-done | bytes 278544 | tf_op jit(solution)/shard_map/psum | solution.py:269
  180.6 1.6 copy.19
  182.2 1.1 copy.24
  183.3 0.0 copy-done.4
  183.3 0.7 copy.25
  184.0 0.0 copy-done.5
  184.0 0.6 copy.26
  (5 shorter events, 0.0 us)
Async XLA Ops:
  7.2 173.4 %all-reduce.3.cloned.1.call-start = ((), (), s32[]{:S(2)}) async-start(), calls=%async_computation | async-start | bytes 983040 | tf_op jit(solution)/shard_map/psum | solution.py:269
  11.2 1.4 copy-start
  12.6 1.4 copy-start.1
  14.1 0.8 copy-start.2
  14.8 0.8 copy-start.3
  182.2 1.1 copy-start.4
  182.2 1.9 copy-start.5
Sparse Core Ops, SparseCore 0:
  51.7 128.8 all-reduce.2

commit v2 on v1

--- a/solution.py
+++ b/solution.py
@@ -34,10 +34,19 @@
     return lax.dot_general(a, b, (((1,), (1,)), ((), ())), preferred_element_type=F32)
 
 
-def kernel(sizes, image, cot, wr, wrt, w2, w3, we, wet, out, g_reduce, g_spatial, g_expand,
+def levels_of(sizes, rows):
+    found = []
+    for axis in ("col", "dp", "row"):
+        count = sizes[axis]
+        rows = -(-rows // (8 * count)) * 8
+        found.append((axis, count, rows))
+    return found
+
+
+def kernel(sizes, scale, image, cot, wr, wrt, w2, w3, we, wet, out, o_reduce, o_spatial, o_expand,
            xin, cin, xf, cf, xb, tb, s1, hid, back, edge, rows_in, cols_in,
-           in_sem, send_sem, recv_sem):
-    nrow, ncol = sizes
+           g_reduce, g_spatial, g_expand, in_sem, send_sem, recv_sem, *sums):
+    nrow, ncol = sizes["row"], sizes["col"]
     channels, height, width = image.shape
     inner = we.shape[0]
     row, col = lax.axis_index("row"), lax.axis_index("col")
@@ -56,13 +65,24 @@
             ok = jnp.logical_and(ok, (col > 0) if dc < 0 else (col < ncol - 1))
         return ok
 
+    def peer_of(axis, count, step):
+        return lax.rem(lax.axis_index(axis) + step, count)
+
     barrier = pltpu.get_barrier_semaphore()
+    greeted = 0
+    for axis, count in sizes.items():
+        for step in range(1, count):
+            pl.semaphore_signal(barrier, inc=1, device_id={axis: peer_of(axis, count, step)},
+                                device_id_type=pl.DeviceIdType.MESH)
+            greeted += 1
     for dr, dc in AROUND:
-        @pl.when(exists(dr, dc))
-        def _(dr=dr, dc=dc):
-            pl.semaphore_signal(barrier, inc=1, device_id={"row": row + dr, "col": col + dc},
-                                device_id_type=pl.DeviceIdType.MESH)
-    pl.semaphore_wait(barrier, sum(exists(dr, dc).astype(jnp.int32) for dr, dc in AROUND))
+        if dr and dc:
+            @pl.when(exists(dr, dc))
+            def _(dr=dr, dc=dc):
+                pl.semaphore_signal(barrier, inc=1, device_id={"row": row + dr, "col": col + dc},
+                                    device_id_type=pl.DeviceIdType.MESH)
+            greeted = greeted + exists(dr, dc).astype(jnp.int32)
+    pl.semaphore_wait(barrier, greeted)
 
     def halo_copy(turn, k, source):
         dr, dc = AROUND[k]
@@ -211,13 +231,77 @@
         pre = dot(w3[...], patch(back, h))
         grad = joined([s1[h + r] for r in range(R)])
         one = (pre * grad).astype(BF16)
-        g_reduce[...] += dot_nt(joined([xb[h + r] for r in range(R)]), one)
+        g_reduce[...] += dot_nt(one, joined([xb[h + r] for r in range(R)]))
         result = dot(wr[...], one) + joined([tb[h + r] for r in range(R)]).astype(F32)
         for r in range(R):
             xf[pl.ds(h + r, channels, stride=height), :] = part(result, r)
         return 0
 
     lax.fori_loop(0, height // R, fourth, 0)
+
+    taps = g_spatial.shape[0] // 2
+    wide = channels // 128
+    total_rows = taps + 2 * wide * inner
+    levels = levels_of(sizes, total_rows)
+    near, far, landed = sums[0:3], sums[3:6], sums[6:9]
+    sems = sums[9:]
+
+    near[0][pl.ds(0, taps)] = joined([g_spatial[pl.ds(0, taps)], g_spatial[pl.ds(taps, taps)]])
+    for k in range(wide):
+        near[0][pl.ds(taps + k * inner, inner)] = g_expand[:, k * 128:(k + 1) * 128]
+        near[0][pl.ds(taps + (wide + k) * inner, inner)] = g_reduce[:, k * 128:(k + 1) * 128]
+    filled = total_rows
+    for level, (axis, count, chunk) in enumerate(levels):
+        if count * chunk > filled:
+            near[level][pl.ds(filled, count * chunk - filled)] = jnp.zeros((count * chunk - filled, 128), F32)
+        filled = chunk
+
+    def send(level, step, gather):
+        axis, count, chunk = levels[level]
+        peer = peer_of(axis, count, step)
+        if gather:
+            mine = pl.ds(pl.multiple_of(lax.axis_index(axis) * chunk, 8), chunk)
+            src, dst = far[level].at[mine], far[level].at[mine]
+        else:
+            src = near[level].at[pl.ds(pl.multiple_of(peer * chunk, 8), chunk)]
+            dst = landed[level].at[step - 1]
+        pair = sems[2 * level + (6 if gather else 0):]
+        return pltpu.make_async_remote_copy(
+            src_ref=src, dst_ref=dst, send_sem=pair[0].at[step - 1], recv_sem=pair[1].at[step - 1],
+            device_id={axis: peer}, device_id_type=pl.DeviceIdType.MESH)
+
+    for level, (axis, count, chunk) in enumerate(levels):
+        copies = [send(level, step, False) for step in range(1, count)]
+        for copy in copies:
+            copy.start()
+        mine = pl.ds(pl.multiple_of(lax.axis_index(axis) * chunk, 8), chunk)
+        value = near[level][mine]
+        for step, copy in enumerate(copies):
+            copy.wait_recv()
+            value = value + landed[level][step]
+        if level < 2:
+            near[level + 1][pl.ds(0, chunk)] = value
+        else:
+            far[level][mine] = value
+        for copy in copies:
+            copy.wait_send()
+    for level in (2, 1, 0):
+        axis, count, chunk = levels[level]
+        if level < 2:
+            far[level][pl.ds(pl.multiple_of(lax.axis_index(axis) * chunk, 8), chunk)] = far[level + 1][pl.ds(0, chunk)]
+        copies = [send(level, step, True) for step in range(1, count)]
+        for copy in copies:
+            copy.start()
+        for step in range(1, count):
+            copies[step - 1].wait_recv()
+        for copy in copies:
+            copy.wait_send()
+    both = far[0][pl.ds(0, taps)] * scale
+    o_spatial[pl.ds(0, taps)] = both[:, :inner]
+    o_spatial[pl.ds(taps, taps)] = both[:, inner:]
+    for k in range(wide):
+        o_expand[:, k * 128:(k + 1) * 128] = far[0][pl.ds(taps + k * inner, inner)] * scale
+        o_reduce[:, k * 128:(k + 1) * 128] = far[0][pl.ds(taps + (wide + k) * inner, inner)] * scale
 
     def narrow(i, _):
         block = xf[pl.ds(pl.multiple_of(i * tiles * height, tiles * height), tiles * height)]
@@ -234,13 +318,14 @@
     scale = float(height * width * count) ** (-0.5)
     w2 = w_spatial.reshape(9 * inner, inner).T
     w3 = jnp.transpose(w_spatial[::-1, ::-1], (2, 0, 1, 3)).reshape(inner, 9 * inner)
+    levels = levels_of(sizes, (9 * inner * inner + 2 * inner * channels) // 128)
     vmem = pl.BlockSpec(memory_space=pltpu.VMEM)
     hbm = pl.BlockSpec(memory_space=pl.ANY)
     result, g_reduce, g_spatial, g_expand = pl.pallas_call(
-        functools.partial(kernel, sizes),
+        functools.partial(kernel, sizes, scale),
         out_shape=(
             jax.ShapeDtypeStruct((channels, height, width), BF16),
-            jax.ShapeDtypeStruct((channels, inner), F32),
+            jax.ShapeDtypeStruct((inner, channels), F32),
             jax.ShapeDtypeStruct((9 * inner, inner), F32),
             jax.ShapeDtypeStruct((inner, channels), F32),
         ),
@@ -259,21 +344,25 @@
             pltpu.VMEM((2, 2, inner, width), F32),
             pltpu.VMEM((2, 2, inner, width), BF16),
             pltpu.VMEM((2, 2, 3, inner, width), F32),
+            pltpu.VMEM((inner, channels), F32),
+            pltpu.VMEM((9 * inner, inner), F32),
+            pltpu.VMEM((inner, channels), F32),
             pltpu.SemaphoreType.DMA((2,)),
             pltpu.SemaphoreType.DMA((2, len(AROUND))),
             pltpu.SemaphoreType.DMA((2, len(AROUND))),
-        ],
+        ] + [pltpu.VMEM((count * chunk, 128), F32) for _, count, chunk in levels]
+        + [pltpu.VMEM((count * chunk, 128), F32) for _, count, chunk in levels]
+        + [pltpu.VMEM((max(count - 1, 1), chunk, 128), F32) for _, count, chunk in levels]
+        + [pltpu.SemaphoreType.DMA((max(count - 1, 1),))
+           for _ in range(2) for _, count, _ in levels for _ in range(2)],
         compiler_params=pltpu.CompilerParams(
             collective_id=0, has_side_effects=True, vmem_limit_bytes=48 * 1024 * 1024),
     )(image[0], cotangent[0], w_reduce, w_reduce.T, w2, w3, w_expand, w_expand.T)
-    g_reduce, g_spatial, g_expand = lax.psum(
-        (g_reduce * scale, g_spatial.reshape(3, 3, inner, inner) * scale, g_expand * scale),
-        ("dp", "row", "col"))
-    return result[None], g_reduce, g_spatial, g_expand
+    return result[None], g_reduce.T, g_spatial.reshape(3, 3, inner, inner), g_expand
 
 
 def solution(mesh):
-    sizes = (mesh.shape["row"], mesh.shape["col"])
+    sizes = {axis: mesh.shape[axis] for axis in ("dp", "row", "col")}
     in_specs = (P("dp", None, "row", "col"), P("dp", None, "row", "col"), P(), P(), P())
     out_specs = (P("dp", None, "row", "col"), P(), P(), P())
     return jax.shard_map(functools.partial(body, sizes), mesh=mesh, in_specs=in_specs,

time: 192 us -> 64.7 us (0.34)
  waiting for transfers between devices: 129 us -> 0 us
  Pallas kernels: 33.9 us -> 52.1 us
  between operations: 14.1 us -> 0.66 us
  other arithmetic: 2.04 us -> 0 us
    psum x1 -> x0, waiting for transfers between devices: 129 us -> none  [body(): lax.psum((g_reduce * scale, g_spatial.reshape(3, 3, inner, inner) * scale...]
    pallas_call x1, Pallas kernels: 33.9 us -> 52.1 us  [body(): pl.pallas_call(functools.partial(kernel, sizes, scale), out_shape=(jax.Sh...]
    mul x3 -> x0, other arithmetic: 2.04 us -> none  [the longest x1 0.74 us: body(): g_spatial.reshape(3, 3, inner, inner) * scale]
    unnamed x18 -> x14, local copies, waits for them, and re-layouts: 10.2 us -> 9.19 us
  transfers between devices with their start and end apart: 1 -> 0, of which waited for: 1 -> 0; matrix products, arithmetic and copies ran while one was open for 0% -> 0% of each run, Pallas kernels for 0% -> 0%
where the time goes in v2:
time: 64.7 us; the launch traced here: 64.2 us
  Pallas kernels  52.1 us (81%)
  local copies, waits for them, and re-layouts  11.5 us (18%)
  between operations  0.66 us (1%)
    pallas_call x1, Pallas kernels, body(): pl.pallas_call(functools.partial(kernel, sizes, scale), out_shape=(jax.Sh...  52.1 us
    unnamed x14, local copies, waits for them, and re-layouts  9.19 us

profile of v2, /device:TPU:0, one launch (start us, length us, event | category | flops | bytes accessed | tf_op | source)
XLA Modules:
  0.0 64.2 jit_solution(12108245013586245340)
XLA Ops:
  0.6 0.9 %copy.16.wr = bf16[256,64]{1,0:T(8,128)(2,1)S(1)} copy(bf16[256,64]{0,1:T(8,128)(2,1)} %param.7) | data formatting | bytes 65536 | tf_op args[2]
  1.5 0.9 %copy.15 = bf16[64,256]{0,1:T(8,128)(2,1)S(1)} copy(bf16[64,256]{1,0:T(8,128)(2,1)} %we.1) | data formatting | bytes 65536 | tf_op args[4]
  2.4 1.0 %copy.13 = bf16[576,64]{0,1:T(8,128)(2,1)S(1)} copy(bf16[576,64]{1,0:T(8,128)(2,1)} %bitcast.20) | data formatting | bytes 147456 | tf_op jit(solution)/shard_map/reshape | solution.py:319
  3.4 0.9 %reverse_bitcast_fusion = bf16[64,3,3,64]{3,0,2,1:T(8,128)(2,1)S(1)} fusion(bf16[3,3,64,64]{3,2,1,0:T(8,128)(2,1)} %param.8), kind=kLoop, calls=%fused_computation | loop fusion | bytes 147456 | tf_op jit(solution)/shard_map/transpose | solution.py:320
  4.4 0.1 copy.14
  4.5 0.1 copy.17.w3
  4.7 0.0 copy-start
  4.7 1.4 %copy-done = bf16[1,256,24,128]{3,2,1,0:T(8,128)(2,1)S(1)} copy-done((bf16[1,256,24,128]{3,2,1,0:T(8,128)(2,1)S(1)}, bf16[1,256,24,128]{3,2,1,0:T(8,128)(2,1)}, u32[]{:S(2)}) %copy-start) | copy-done | bytes 1572888
  6.1 0.0 copy-start.1
  6.1 1.4 %copy-done.1 = bf16[1,256,24,128]{3,2,1,0:T(8,128)(2,1)S(1)} copy-done((bf16[1,256,24,128]{3,2,1,0:T(8,128)(2,1)S(1)}, bf16[1,256,24,128]{3,2,1,0:T(8,128)(2,1)}, u32[]{:S(2)}) %copy-start.1) | copy-done | bytes 1572888
  7.5 0.0 copy-start.2
  7.5 0.8 %copy-done.2 = bf16[256,64]{0,1:T(8,128)(2,1)S(1)} copy-done((bf16[256,64]{0,1:T(8,128)(2,1)S(1)}, bf16[256,64]{0,1:T(8,128)(2,1)}, u32[]{:S(2)}) %copy-start.2) | copy-done | bytes 32792
  8.2 0.0 copy-start.3
  8.2 0.8 %copy-done.3 = bf16[64,256]{1,0:T(8,128)(2,1)S(1)} copy-done((bf16[64,256]{1,0:T(8,128)(2,1)S(1)}, bf16[64,256]{1,0:T(8,128)(2,1)}, u32[]{:S(2)}) %copy-start.3) | copy-done | bytes 32792
  9.0 52.1 %shard_map.84 = (bf16[256,24,128]{2,1,0:T(8,128)(2,1)S(1)}, f32[64,256]{1,0:T(8,128)S(1)}, f32[576,64]{1,0:T(8,128)S(1)}, f32[64,256]{1,0:T(8,128)S(1)}) custom-call(bf16[256,24,128]{2,1,0:T(8,128)(2,1)S(1)} %bitcast.12, bf16[256,24,128]{2,1,0:T(8,128)(2,1)S(1)} %bitcast.13, bf16[256,64]{1,0:T(8,128)(2,1)S(1)} %copy.16.wr, bf16[64,256]{1,0:T(8,128)(2,1)S(1)} %bitcast.18, ...), custom_call_target="tpu_custom_call" | custom-call | tf_op jit(solution)/shard_map/pallas_call | solution.py:324
  61.1 1.1 %copy.22 = bf16[1,256,24,128]{3,2,1,0:T(8,128)(2,1)} copy(bf16[1,256,24,128]{3,2,1,0:T(8,128)(2,1)S(1)} %bitcast.14) | data formatting | bytes 3145728
  62.2 0.6 copy.23
  62.9 0.7 %copy.24 = f32[3,3,64,64]{3,2,1,0:T(8,128)} copy(f32[3,3,64,64]{3,2,1,0:T(8,128)S(1)} %bitcast.16) | data formatting | bytes 294912
  63.6 0.6 copy.25
Async XLA Ops:
  4.7 1.4 %copy-start = (bf16[1,256,24,128]{3,2,1,0:T(8,128)(2,1)S(1)}, bf16[1,256,24,128]{3,2,1,0:T(8,128)(2,1)}, u32[]{:S(2)}) copy-start(bf16[1,256,24,128]{3,2,1,0:T(8,128)(2,1)} %param.5) | copy-start | bytes 4718596
  6.1 1.4 %copy-start.1 = (bf16[1,256,24,128]{3,2,1,0:T(8,128)(2,1)S(1)}, bf16[1,256,24,128]{3,2,1,0:T(8,128)(2,1)}, u32[]{:S(2)}) copy-start(bf16[1,256,24,128]{3,2,1,0:T(8,128)(2,1)} %param.6) | copy-start | bytes 4718596
  7.5 0.8 %copy-start.2 = (bf16[256,64]{0,1:T(8,128)(2,1)S(1)}, bf16[256,64]{0,1:T(8,128)(2,1)}, u32[]{:S(2)}) copy-start(bf16[256,64]{0,1:T(8,128)(2,1)} %param.7) | copy-start | bytes 98308
  8.2 0.8 %copy-start.3 = (bf16[64,256]{1,0:T(8,128)(2,1)S(1)}, bf16[64,256]{1,0:T(8,128)(2,1)}, u32[]{:S(2)}) copy-start(bf16[64,256]{1,0:T(8,128)(2,1)} %we.1) | copy-start | bytes 98308
